TPU v7x, 32 devices: a whole 2x2x4 slice. The times are simulated.
32 devices in a mesh: index: 8 (over y, x, core), query: 4 (over z).
Axes of the slice: x: 2, y: 2, z: 4, core: 2. Of those that a mesh axis runs over, the one named last changes fastest.
Arguments:
- queries: bfloat16 [256, 2048], P(('index', 'query')), may hold values from -4 to 4
- slab: bfloat16 [131072, 2048], P(('index', 'query')), may hold values from -24 to 24
- cand_owner: int32 [256, 32], P(('index', 'query')), may hold values from 0 to 31, all different within a row; in each aligned block of 8 rows (0 to 7, 8 to 15, ...) at most 8 rows name the same one
- cand_row: int32 [256, 32], P(('index', 'query')), may hold values from 0 to 4095
Outputs:
- pooled: float32 [256, 256], P(('index', 'query'))
- coarse_lse: float32 [256], P(('index', 'query'))
- margin: float32 [256, 32], P(('index', 'query'))
Inputs may be any that keep to these rules, and one draw needn't show every extreme that they name: `cand_owner`: each query names 32 distinct owners. Over the 8 queries of one device (aligned blocks of 8 rows) no owner is named more than 8 times, a bound that some block reaches.
All inputs are finite; a program needn't handle non-finite values.
Results may differ from a plain program's by a relative error of at most 0.00165.
Values may be sent and summed in bfloat16 or wider, within the bound.
No kernel may reach another device: no remote copies, remote signals or barrier semaphores. Data moves between devices by JAX's collectives and lax.ppermute only.
A program may use at most 128 MiB of HBM per device.

v0:
```python
import jax
import jax.numpy as jnp
from jax import lax
from jax.sharding import PartitionSpec as P

PREFIX = 256


def on_device(queries, slab, cand_owner, cand_row):
    q_dev = queries.shape[0]
    width = slab.shape[1]
    owners = lax.axis_size(("index", "query"))
    k_count = cand_owner.shape[1]
    prefix_keys = slab[:, :PREFIX]
    scale = PREFIX ** (-0.5)
    logits = (
        lax.dot_general(
            lax.all_gather(queries[:, :PREFIX], ("index", "query"), axis=0, tiled=True),
            prefix_keys,
            (((1,), (1,)), ((), ())),
            preferred_element_type=jnp.float32,
        )
        * scale
    )
    top = lax.pmax(jnp.max(logits, axis=1), ("index", "query"))
    weights = jnp.exp(logits - top[:, None])
    parts = (
        jnp.dot(weights.astype(jnp.bfloat16), prefix_keys, preferred_element_type=jnp.float32),
        jnp.sum(weights, axis=1),
    )
    results = lax.psum_scatter(parts, ("index", "query"), scatter_dimension=0, tiled=True)
    pooled_sum = results[0]
    total = results[1]
    my_start = lax.axis_index(("index", "query")) * q_dev
    my_top = lax.dynamic_slice_in_dim(top, my_start, q_dev, 0)
    pooled = pooled_sum / total[:, None]
    coarse_lse = my_top + jnp.log(total)
    capacity = max(2, min(q_dev, 2 * q_dev * k_count // owners))
    flat_owner = cand_owner.reshape(-1)
    flat_row = cand_row.reshape(-1)
    hits = (flat_owner[:, None] == jnp.arange(owners, dtype=jnp.int32)[None, :]).astype(jnp.int32)
    earlier = jnp.cumsum(hits, axis=0) - hits
    slot = jnp.sum(earlier * hits, axis=1)
    target = flat_owner * capacity + slot
    request = jnp.zeros((owners * capacity,), jnp.int32).at[target].set(flat_row)
    fetched = lax.all_to_all(
        slab[
            lax.all_to_all(
                request.reshape(owners, capacity),
                ("index", "query"),
                split_axis=0,
                concat_axis=0,
                tiled=True,
            )
        ],
        ("index", "query"),
        split_axis=0,
        concat_axis=0,
        tiled=True,
    )
    cand_rows = fetched.reshape(owners * capacity, width)[target].reshape(q_dev, k_count, width)
    full = jnp.einsum(
        "qw,qkw->qk", queries, cand_rows, preferred_element_type=jnp.float32
    ) * width ** (-0.5)
    margin = full - coarse_lse[:, None]
    return (pooled, coarse_lse, margin)


def solution(mesh):
    in_specs = (
        P(("index", "query"), None),
        P(("index", "query"), None),
        P(("index", "query"), None),
        P(("index", "query"), None),
    )
    out_specs = (P(("index", "query"), None), P(("index", "query")), P(("index", "query"), None))
    return jax.shard_map(
        on_device, mesh=mesh, in_specs=in_specs, out_specs=out_specs, check_vma=False
    )
```

profile of v0, /device:TPU:0, one launch (start us, length us, event | category | flops | bytes accessed | tf_op | source)
XLA Modules:
  0.0 318.5 jit_solution(5790546167381804350)
XLA Ops:
  7.2 0.8 eq.29
  7.9 0.8 eq.25
  8.7 0.7 broadcast_multiply_fusion
  9.4 0.8 reshape.120
  10.1 0.1 mul.43
  10.2 0.6 reduce-window.6
  10.8 0.2 slice_reduce_fusion
  11.1 0.1 fusion.11
  11.2 1.4 scatter_custom_fusion
  12.6 0.1 all_to_all.11
  12.7 14.3 %all_to_all.17 = s32[32,1,8]{2,1,0:T(1,128)S(1)} all-to-all(s32[32,1,8]{2,1,0:T(1,128)S(1)} %bitcast.36), channel_id=1, replica_groups=mesh['index'=8,'query'=4] {'index','query'}, dimensions={0} | all-to-all | bytes 2048 | tf_op jit(solution)/shard_map/all_to_all | solution.py:48
  27.0 0.1 reshape.102
  27.1 0.0 slice-start
  27.1 11.3 %gather_fusion = bf16[256,2048]{1,0:T(8,128)(2,1)} fusion(bf16[4096,2048]{1,0:T(8,128)(2,1)} %param.5, s32[1024]{0:T(1024)S(1)} %pad_clamp_fusion.1), kind=kCustom, calls=%fused_computation | custom fusion | bytes 2098176 | tf_op jit(solution)/shard_map/gather | solution.py:47
  38.4 2.6 all-to-all-start.1
  41.0 0.0 reduce-scatter.2.cloned.1.call-start
  41.1 0.0 slice-done
  41.1 84.3 %all_gather.3 = bf16[256,256]{1,0:T(8,128)(2,1)S(1)} all-gather(bf16[8,256]{1,0:T(8,128)(2,1)S(1)} %slice-done), channel_id=1, replica_groups=mesh['index'=8,'query'=4] {'index','query'}, dimensions={0}, use_global_device_ids=true | all-gather | bytes 135168 | tf_op jit(solution)/shard_map/all_gather | solution.py:18
  125.4 4.3 %fusion.15 = (f32[256]{0:T(256)S(1)}, f32[256,4096]{1,0:T(8,128)}) fusion(bf16[256,256]{1,0:T(8,128)(2,1)S(1)} %all_gather.3, bf16[4096,2048]{1,0:T(8,128)(2,1)} %param.5), kind=kOutput, calls=%fused_computation.32 | convolution fusion | flops 538967808 | bytes 6423552 | tf_op jit(solution)/shard_map/dot_general | solution.py:17
  129.6 36.8 %pmax.7 = f32[256]{0:T(256)S(1)} all-reduce(f32[256]{0:T(256)S(1)} %get-tuple-element.5), channel_id=1, replica_groups=mesh['index'=8,'query'=4] {'index','query'}, use_global_device_ids=true, to_apply=%region_1.0 | all-reduce | flops 256 | bytes 2048 | tf_op jit(solution)/shard_map/pmax | solution.py:25
  166.4 4.3 %fusion.2 = f32[256,256]{1,0:T(8,128)} fusion(f32[256,4096]{1,0:T(8,128)} %get-tuple-element.6, f32[256]{0:T(256)S(1)} %pmax.7, bf16[4096,2048]{1,0:T(8,128)(2,1)} %param.5), kind=kOutput, calls=%fused_computation.7 | convolution fusion | flops 538968064 | bytes 6554624 | tf_op jit(solution)/shard_map/dot_general | solution.py:28
  170.8 0.0 reduce-scatter.2.cloned.1.call-update
  170.8 2.9 fusion
  173.7 42.3 %all-reduce = f32[256]{0:T(256)S(1)} all-reduce(f32[256]{0:T(256)S(1)} %fusion), channel_id=3, replica_groups=mesh['index'=8,'query'=4] {'index','query'}, use_global_device_ids=true, to_apply=%region_4.0.clone | all-reduce | flops 256 | bytes 2048
  216.0 0.1 log_add_fusion
  216.0 91.8 %reduce-scatter.2.cloned.1.call-done = f32[8,256]{1,0:T(8,128)} async-done(((f32[256,256]{1,0:T(8,128)}), f32[8,256]{1,0:T(8,128)}) %reduce-scatter.2.cloned.1.call-update) | async-done | bytes 8208 | tf_op jit(solution)/shard_map/reduce_scatter | solution.py:31
  307.9 1.4 broadcast_divide_fusion
  309.2 0.0 all-to-all-done.1
  309.3 1.4 gather_fusion.1
  310.6 0.0 copy-done
  310.6 0.4 fusion.7
  311.0 0.7 multiply_subtract_fusion
  (10 shorter events, 0.1 us)
Async XLA Ops:
  27.1 14.0 %slice-start = ((bf16[8,2048]{1,0:T(8,128)(2,1)}), bf16[8,256]{1,0:T(8,128)(2,1)S(1)}, s32[]{:S(2)}) async-start(bf16[8,2048]{1,0:T(8,128)(2,1)} %param.4), calls=%async_computation.4 | async-start | bytes 8192 | tf_op jit(solution)/shard_map/slice | solution.py:18
  38.4 270.9 %all-to-all-start.1 = ((bf16[32,8,2048]{2,1,0:T(8,128)(2,1)}), bf16[32,8,2048]{2,1,0:T(8,128)(2,1)S(1)}, u32[]{:S(2)}, u32[]{:S(2)}) async-start(bf16[32,8,2048]{2,1,0:T(8,128)(2,1)} %bitcast.5), calls=%async_computation.2 | async-start | bytes 2097152 | tf_op jit(solution)/shard_map/all_to_all | solution.py:46
  41.0 266.8 %reduce-scatter.2.cloned.1.call-start = ((), (), s32[]{:S(2)}) async-start(), calls=%async_computation.3 | async-start | bytes 270336 | tf_op jit(solution)/shard_map/reduce_scatter | solution.py:31
  216.0 95.0 %copy-start.1 = (f32[8]{0:T(128)}, f32[8]{0:T(128)S(1)}, u32[]{:S(2)}) copy-start(f32[8]{0:T(128)S(1)} %get-tuple-element.3) | copy-start | bytes 100
  309.2 1.4 copy-start
Sparse Core Ops, SparseCore 0:
  170.9 136.9 reduce-scatter.1
where the time goes:
time: 319 us
  blocking collectives  178 us (56%)
  waiting for transfers between devices  91.9 us (29%)
  local copies, waits for them, and re-layouts  16.8 us (5%)
  between operations  14.1 us (4%)
  matrix products  8.96 us (3%)
  other arithmetic  6.46 us (2%)
    reduce_scatter x1, waiting for transfers between devices, on_device(): lax.psum_scatter(parts, ('index', 'query'), scatter_dimension=0, tiled=True)  91.8 us
    all_gather x1, blocking collectives, on_device(): lax.all_gather(queries[:, :PREFIX], ('index', 'query'), axis=0, tiled=True)  84.3 us
    unnamed x1, blocking collectives  42.3 us
    pmax x1, blocking collectives, on_device(): top = lax.pmax(jnp.max(logits, axis=1), ('index', 'query'))  36.8 us
    all_to_all x1, blocking collectives, on_device(): lax.all_to_all(request.reshape(owners, capacity), ('index', 'query'), spl...  14.3 us
    gather x1, local copies, waits for them, and re-layouts, on_device(): slab[lax.all_to_all(request.reshape(owners, capacity), ('index', 'query')...  11.3 us
  transfers between devices with their start and end apart: 2, of which 1 were waited for; matrix products, arithmetic and copies ran while one was open for 4% of the time, Pallas kernels for 0%

commit v1 on v0

--- a/solution.py
+++ b/solution.py
@@ -4,6 +4,29 @@
 from jax.sharding import PartitionSpec as P
 
 PREFIX = 256
+
+
+def in_order(blocks, dim):
+    shape = list(blocks.shape[1:])
+    shape[dim] *= blocks.shape[0]
+    return jnp.moveaxis(blocks, 0, dim).reshape(shape)
+
+
+def collected_by_bits(value, axis):
+    length, index = (lax.axis_size(axis), lax.axis_index(axis))
+    pieces, bit = (value[None], 1)
+    while bit < length:
+        received = lax.ppermute(pieces, axis, [(i, i ^ bit) for i in range(length)])
+        low = index & bit == 0
+        pieces = jnp.concatenate(
+            [jnp.where(low, pieces, received), jnp.where(low, received, pieces)]
+        )
+        bit *= 2
+    return pieces
+
+
+def gather_by_bits(x, axis, dim):
+    return in_order(collected_by_bits(x, axis), dim)
 
 
 def on_device(queries, slab, cand_owner, cand_row):
@@ -15,7 +38,7 @@
     scale = PREFIX ** (-0.5)
     logits = (
         lax.dot_general(
-            lax.all_gather(queries[:, :PREFIX], ("index", "query"), axis=0, tiled=True),
+            gather_by_bits(queries[:, :PREFIX], ("index", "query"), 0),
             prefix_keys,
             (((1,), (1,)), ((), ())),
             preferred_element_type=jnp.float32,

time: 319 us -> 252 us (0.79)
  blocking collectives: 178 us -> 79.7 us
  waiting for transfers between devices: 91.9 us -> 109 us
  starting transfers between devices: 2.69 us -> 13.8 us
    all_gather x1 -> x0, blocking collectives: 84.3 us -> none  [on_device(): lax.all_gather(queries[:, :PREFIX], ('index', 'query'), axis=0, tiled=True)]
    all_to_all x1 -> x0, blocking collectives: 14.3 us -> none  [on_device(): lax.all_to_all(request.reshape(owners, capacity), ('index', 'query'), spl...]
    ppermute x0 -> x5, waiting for transfers between devices: none -> 9.55 us  [collected_by_bits(): received = lax.ppermute(pieces, axis, [(i, i ^ bit) for i in range(length)])]
    ppermute x0 -> x5, starting transfers between devices: none -> 8.33 us  [collected_by_bits(): received = lax.ppermute(pieces, axis, [(i, i ^ bit) for i in range(length)])]
    all_to_all x0 -> x1, waiting for transfers between devices: none -> 6.82 us  [on_device(): lax.all_to_all(request.reshape(owners, capacity), ('index', 'query'), spl...]
  transfers between devices with their start and end apart: 2 -> 8, of which waited for: 1 -> 3; matrix products, arithmetic and copies ran while one was open for 4% -> 12% of each run, Pallas kernels for 0% -> 0%
where the time goes in v1:
time: 252 us; the launch traced here: 251 us
  waiting for transfers between devices  109 us (43%)
  blocking collectives  79.7 us (32%)
  local copies, waits for them, and re-layouts  18 us (7%)
  between operations  14.2 us (6%)
  starting transfers between devices  13.8 us (5%)
  matrix products  8.97 us (4%)
  other arithmetic  7.23 us (3%)
    reduce_scatter x1, waiting for transfers between devices, on_device(): lax.psum_scatter(parts, ('index', 'query'), scatter_dimension=0, tiled=True)  92.4 us
    unnamed x1, blocking collectives  40.7 us
    pmax x1, blocking collectives, on_device(): top = lax.pmax(jnp.max(logits, axis=1), ('index', 'query'))  39 us
    gather x1, local copies, waits for them, and re-layouts, on_device(): slab[lax.all_to_all(request.reshape(owners, capacity), ('index', 'query')...  11.3 us
    ppermute x5, waiting for transfers between devices, collected_by_bits(): received = lax.ppermute(pieces, axis, [(i, i ^ bit) for i in range(length)])  9.55 us
    ppermute x5, starting transfers between devices, collected_by_bits(): received = lax.ppermute(pieces, axis, [(i, i ^ bit) for i in range(length)])  8.33 us
    all_to_all x1, waiting for transfers between devices, on_device(): lax.all_to_all(request.reshape(owners, capacity), ('index', 'query'), spl...  6.82 us
  transfers between devices with their start and end apart: 8, of which 3 were waited for; matrix products, arithmetic and copies ran while one was open for 12% of the time, Pallas kernels for 0%

profile of v1, /device:TPU:0, one launch (start us, length us, event | category | flops | bytes accessed | tf_op | source)
XLA Modules:
  0.0 250.8 jit_solution(4562514205227753045)
XLA Ops:
  7.2 0.7 slice_bitcast_fusion
  7.9 3.1 %collective-permute-start = (bf16[1,8,256]{2,1,0:T(8,128)(2,1)S(1)}, bf16[1,8,256]{2,1,0:T(8,128)(2,1)S(1)}, u32[]{:S(2)}, u32[]{:S(2)}) collective-permute-start(bf16[1,8,256]{2,1,0:T(8,128)(2,1)S(1)} %slice_bitcast_fusion), channel_id=1, source_target_pairs={{0,1},{1,0},{2,3},{3,2},{4,5},{5,4},{6,7},{7,6},{8,9},{9,8},{10,11... | collective-permute-start | bytes 12296 | tf_op jit(solution)/shard_map/ppermute | solution.py:19
  10.9 0.8 eq.49
  11.7 0.8 eq.45
  12.4 0.7 broadcast_multiply_fusion
  13.1 0.6 reduce-window.6
  13.7 0.2 slice_reduce_fusion
  13.9 0.1 fusion.13
  14.1 0.7 broadcast_select_fusion.9
  14.8 2.6 %collective-permute-start.1 = (bf16[2,8,256]{2,1,0:T(8,128)(2,1)S(1)}, bf16[2,8,256]{2,1,0:T(8,128)(2,1)S(1)}, u32[]{:S(2)}, u32[]{:S(2)}) collective-permute-start(bf16[2,8,256]{2,1,0:T(8,128)(2,1)S(1)} %pad_maximum_fusion.3), channel_id=1, source_target_pairs={{0,2},{1,3},{2,0},{3,1},{4,6},{5,7},{6,4},{7,5},{8,10},{9,11},{10,... | collective-permute-start | bytes 24584 | tf_op jit(solution)/shard_map/ppermute | solution.py:19
  17.4 0.8 reshape.124
  18.2 1.4 scatter_custom_fusion
  19.6 0.7 all_to_all.11
  20.3 2.8 %all-to-all-start = ((s32[32,1,8]{2,1,0:T(1,128)}), s32[32,1,8]{2,1,0:T(1,128)S(1)}, u32[]{:S(2)}, u32[]{:S(2)}) async-start(s32[32,1,8]{2,1,0:T(1,128)} %bitcast.5), calls=%async_computation.1 | async-start | bytes 32768 | tf_op jit(solution)/shard_map/all_to_all | solution.py:71
  23.2 0.3 collective-permute-start.2
  23.5 6.8 %all-to-all-done = s32[32,1,8]{2,1,0:T(1,128)S(1)} async-done(((s32[32,1,8]{2,1,0:T(1,128)}), s32[32,1,8]{2,1,0:T(1,128)S(1)}, u32[]{:S(2)}, u32[]{:S(2)}) %all-to-all-start) | async-done | bytes 1056 | tf_op jit(solution)/shard_map/all_to_all | solution.py:71
  30.3 0.1 reshape.106
  30.4 0.7 collective-permute-start.3
  31.1 11.3 %gather_fusion = bf16[256,2048]{1,0:T(8,128)(2,1)} fusion(bf16[4096,2048]{1,0:T(8,128)(2,1)} %param.5, s32[1024]{0:T(1024)S(1)} %pad_clamp_fusion.1), kind=kCustom, calls=%fused_computation | custom fusion | bytes 2098176 | tf_op jit(solution)/shard_map/gather | solution.py:70
  42.4 2.6 %all-to-all-start.1 = ((bf16[32,8,2048]{2,1,0:T(8,128)(2,1)}), bf16[32,8,2048]{2,1,0:T(8,128)(2,1)S(1)}, u32[]{:S(2)}, u32[]{:S(2)}) async-start(bf16[32,8,2048]{2,1,0:T(8,128)(2,1)} %bitcast.7), calls=%async_computation.2 | async-start | bytes 2097152 | tf_op jit(solution)/shard_map/all_to_all | solution.py:69
  45.1 1.7 collective-permute-start.4
  46.8 9.5 %collective-permute-done.4 = bf16[16,8,256]{2,1,0:T(8,128)(2,1)S(1)} collective-permute-done((bf16[16,8,256]{2,1,0:T(8,128)(2,1)S(1)}, bf16[16,8,256]{2,1,0:T(8,128)(2,1)S(1)}, u32[]{:S(2)}, u32[]{:S(2)}) %collective-permute-start.4) | collective-permute-done | bytes 65568 | tf_op jit(solution)/shard_map/ppermute | solution.py:19
  56.4 4.3 %fusion.18 = (f32[256]{0:T(256)S(1)}, f32[256,4096]{1,0:T(8,128)}) fusion(bf16[4096,2048]{1,0:T(8,128)(2,1)} %param.5, bf16[16,8,256]{2,1,0:T(8,128)(2,1)S(1)} %get-tuple-element.6, bf16[16,8,256]{2,1,0:T(8,128)(2,1)S(1)} %get-tuple-element.5), kind=kOutput, calls=%fused_computation.51 | convolution fusion | flops 539033344 | bytes 6423552 | tf_op jit(solution)/shard_map/dot_general | solution.py:40
  60.6 39.0 %pmax.7 = f32[256]{0:T(256)S(1)} all-reduce(f32[256]{0:T(256)S(1)} %get-tuple-element.15), channel_id=1, replica_groups=mesh['index'=8,'query'=4] {'index','query'}, use_global_device_ids=true, to_apply=%region_1.2 | all-reduce | flops 256 | bytes 2048 | tf_op jit(solution)/shard_map/pmax | solution.py:48
  99.7 4.3 %fusion.2 = f32[256,256]{1,0:T(8,128)} fusion(f32[256,4096]{1,0:T(8,128)} %get-tuple-element.16, f32[256]{0:T(256)S(1)} %pmax.7, bf16[4096,2048]{1,0:T(8,128)(2,1)} %param.5), kind=kOutput, calls=%fused_computation.7 | convolution fusion | flops 538968064 | bytes 6554624 | tf_op jit(solution)/shard_map/dot_general | solution.py:51
  104.1 2.9 %fusion = f32[256]{0:T(256)S(1)} fusion(f32[256,4096]{1,0:T(8,128)} %get-tuple-element.16, f32[256]{0:T(256)S(1)} %pmax.7), kind=kLoop, calls=%fused_computation.5 | loop fusion | flops 2096896 | bytes 4196352 | tf_op jit(solution)/shard_map/reduce_sum | solution.py:52
  107.0 40.7 %all-reduce = f32[256]{0:T(256)S(1)} all-reduce(f32[256]{0:T(256)S(1)} %fusion), channel_id=3, replica_groups=mesh['index'=8,'query'=4] {'index','query'}, use_global_device_ids=true, to_apply=%region_4.5.clone | all-reduce | flops 256 | bytes 2048
  147.7 92.4 %reduce-scatter.2.cloned.1.call-done = f32[8,256]{1,0:T(8,128)} async-done(((f32[256,256]{1,0:T(8,128)}), f32[8,256]{1,0:T(8,128)}) %reduce-scatter.2.cloned.1.call-update) | async-done | bytes 8208 | tf_op jit(solution)/shard_map/reduce_scatter | solution.py:54
  240.2 1.4 broadcast_divide_fusion
  241.5 1.4 gather_fusion.1
  242.9 0.4 fusion.9
  243.3 0.7 multiply_subtract_fusion
  (28 shorter events, 0.4 us)
Async XLA Ops:
  7.9 6.3 %collective-permute-start = (bf16[1,8,256]{2,1,0:T(8,128)(2,1)S(1)}, bf16[1,8,256]{2,1,0:T(8,128)(2,1)S(1)}, u32[]{:S(2)}, u32[]{:S(2)}) collective-permute-start(bf16[1,8,256]{2,1,0:T(8,128)(2,1)S(1)} %slice_bitcast_fusion), channel_id=1, source_target_pairs={{0,1},{1,0},{2,3},{3,2},{4,5},{5,4},{6,7},{7,6},{8,9},{9,8},{10,11... | collective-permute-start | bytes 12296 | tf_op jit(solution)/shard_map/ppermute | solution.py:19
  14.8 8.3 %collective-permute-start.1 = (bf16[2,8,256]{2,1,0:T(8,128)(2,1)S(1)}, bf16[2,8,256]{2,1,0:T(8,128)(2,1)S(1)}, u32[]{:S(2)}, u32[]{:S(2)}) collective-permute-start(bf16[2,8,256]{2,1,0:T(8,128)(2,1)S(1)} %pad_maximum_fusion.3), channel_id=1, source_target_pairs={{0,2},{1,3},{2,0},{3,1},{4,6},{5,7},{6,4},{7,5},{8,10},{9,11},{10,... | collective-permute-start | bytes 24584 | tf_op jit(solution)/shard_map/ppermute | solution.py:19
  20.3 10.0 %all-to-all-start = ((s32[32,1,8]{2,1,0:T(1,128)}), s32[32,1,8]{2,1,0:T(1,128)S(1)}, u32[]{:S(2)}, u32[]{:S(2)}) async-start(s32[32,1,8]{2,1,0:T(1,128)} %bitcast.5), calls=%async_computation.1 | async-start | bytes 32768 | tf_op jit(solution)/shard_map/all_to_all | solution.py:71
  23.2 7.2 %collective-permute-start.2 = (bf16[4,8,256]{2,1,0:T(8,128)(2,1)S(1)}, bf16[4,8,256]{2,1,0:T(8,128)(2,1)S(1)}, u32[]{:S(2)}, u32[]{:S(2)}) collective-permute-start(bf16[4,8,256]{2,1,0:T(8,128)(2,1)S(1)} %pad_maximum_fusion.2), channel_id=1, source_target_pairs={{0,4},{1,5},{2,6},{3,7},{4,0},{5,1},{6,2},{7,3},{8,12},{9,13},{10,... | collective-permute-start | bytes 49160 | tf_op jit(solution)/shard_map/ppermute | solution.py:19
  30.4 14.6 %collective-permute-start.3 = (bf16[8,8,256]{2,1,0:T(8,128)(2,1)S(1)}, bf16[8,8,256]{2,1,0:T(8,128)(2,1)S(1)}, u32[]{:S(2)}, u32[]{:S(2)}) collective-permute-start(bf16[8,8,256]{2,1,0:T(8,128)(2,1)S(1)} %pad_maximum_fusion.1), channel_id=1, source_target_pairs={{0,8},{1,9},{2,10},{3,11},{4,12},{5,13},{6,14},{7,15},{8,0},{9,1},... | collective-permute-start | bytes 98312 | tf_op jit(solution)/shard_map/ppermute | solution.py:19
  42.4 199.2 %all-to-all-start.1 = ((bf16[32,8,2048]{2,1,0:T(8,128)(2,1)}), bf16[32,8,2048]{2,1,0:T(8,128)(2,1)S(1)}, u32[]{:S(2)}, u32[]{:S(2)}) async-start(bf16[32,8,2048]{2,1,0:T(8,128)(2,1)} %bitcast.7), calls=%async_computation.2 | async-start | bytes 2097152 | tf_op jit(solution)/shard_map/all_to_all | solution.py:69
  45.0 195.2 %reduce-scatter.2.cloned.1.call-start = ((), (), s32[]{:S(2)}) async-start(), calls=%async_computation.3 | async-start | bytes 270336 | tf_op jit(solution)/shard_map/reduce_scatter | solution.py:54
  45.1 11.3 %collective-permute-start.4 = (bf16[16,8,256]{2,1,0:T(8,128)(2,1)S(1)}, bf16[16,8,256]{2,1,0:T(8,128)(2,1)S(1)}, u32[]{:S(2)}, u32[]{:S(2)}) collective-permute-start(bf16[16,8,256]{2,1,0:T(8,128)(2,1)S(1)} %pad_maximum_fusion), channel_id=1, source_target_pairs={{0,16},{1,17},{2,18},{3,19},{4,20},{5,21},{6,22},{7,23},{8,24},{9,... | collective-permute-start | bytes 196616 | tf_op jit(solution)/shard_map/ppermute | solution.py:19
  147.7 95.6 %copy-start = (f32[8]{0:T(128)}, f32[8]{0:T(128)S(1)}, u32[]{:S(2)}) copy-start(f32[8]{0:T(128)S(1)} %get-tuple-element.3) | copy-start | bytes 100
  241.5 1.4 copy-start.1
Sparse Core Ops, SparseCore 0:
  104.2 135.9 reduce-scatter.1
